TPU v7x, 32 devices: a whole 2x2x4 slice. The times are simulated.
32 devices in a mesh: outer: 4 (over y, x), inner: 2 (over core), col: 4 (over z).
Axes of the slice: x: 2, y: 2, z: 4, core: 2. Of those that a mesh axis runs over, the one named last changes fastest.
Arguments:
- operator: bfloat16 [4096, 8192], P(('outer', 'inner'), 'col'), as said below
- test_matrix: bfloat16 [8192, 256], P('col'), may hold values from -6 to 6
Outputs:
- basis: float32 [4096, 256], P(('outer', 'inner'), 'col')
- factor: float32 [256, 256], replicated
Inputs may be any that keep to these rules, and one draw needn't show every extreme that they name: Entries of the operator are of order 1 / sqrt(8192) times row and column scales between 0.5 and 4.
All inputs are finite; a program needn't handle non-finite values.
Results may differ from a plain program's by a relative error of at most 0.003.
Values may be sent and summed in bfloat16 or wider, within the bound.
A program may use at most 64 MiB of HBM per device.

v0:
```python
import jax
import jax.numpy as jnp
from jax import lax
from jax.sharding import PartitionSpec as P


def right_solve(lower, matrix):
    return jax.scipy.linalg.solve_triangular(lower, matrix.T, lower=True).T


def transposed_product(block, sketch):
    return lax.dot_general(
        block, sketch, (((0,), (0,)), ((), ())), preferred_element_type=jnp.float32
    )


def shards(operator, test_matrix):
    row_groups = lax.axis_size("outer") * lax.axis_size("inner")
    col_groups = lax.axis_size("col")
    local_cols = operator.shape[1]
    total_rows = operator.shape[0] * row_groups
    total_cols = local_cols * col_groups
    ratio = total_cols / total_rows
    partial_sketch = jnp.dot(operator, test_matrix, preferred_element_type=jnp.float32)
    sketch = lax.psum(partial_sketch, "col").astype(jnp.bfloat16)
    partial_normal = transposed_product(operator, sketch)
    summed = lax.psum(partial_normal, ("outer", "inner"))
    normal = (summed * ratio).astype(jnp.bfloat16)
    partial_image = jnp.dot(operator, normal, preferred_element_type=jnp.float32)
    image = lax.psum(partial_image, "col")
    local_gram = jnp.dot(
        image.T, image, precision=lax.Precision.HIGHEST, preferred_element_type=jnp.float32
    )
    gram = lax.psum(local_gram, ("outer", "inner"))
    lower = jnp.linalg.cholesky(gram)
    width = image.shape[1] // col_groups
    orthonormal = right_solve(lower, image)
    root = jnp.sqrt(jnp.float32(total_rows))
    basis = lax.dynamic_slice_in_dim(orthonormal, lax.axis_index("col") * width, width, 1) * root
    factor = lower.T / root
    return (basis, factor)


def solution(mesh):
    placed = (P(("outer", "inner"), "col"), P("col", None))
    return jax.shard_map(
        shards,
        mesh=mesh,
        in_specs=placed,
        out_specs=(P(("outer", "inner"), "col"), P()),
        check_vma=False,
    )
```

profile of v0, /device:TPU:0, one launch (start us, length us, event | category | flops | bytes accessed | tf_op | source)
XLA Modules:
  0.0 275.8 jit_solution(421812006087493749)
XLA Ops:
  7.2 0.0 copy-start
  7.2 0.0 all-reduce.6.cloned.1.call-start
  7.2 1.5 copy-done
  8.8 1.9 fusion.16
  10.7 32.1 %all-reduce.11 = bf16[512,256]{1,0:T(8,128)(2,1)S(1)} all-reduce(f32[512,256]{1,0:T(8,128)S(1)} %fusion.16), channel_id=1, replica_groups=mesh['outer'=4,'inner'=2,'col'=4] {'col'}, use_global_device_ids=true, to_apply=%region_0.0 | all-reduce | flops 131072 | bytes 786432 | tf_op jit(solution)/shard_map/psum | solution.py:25
  42.8 2.0 convolution_bitcast_fusion
  44.8 0.0 all-reduce.6.cloned.1.call-update
  44.9 0.0 all-reduce.8.cloned.1.call-start
  44.9 60.1 %all-reduce.6.cloned.1.call-done = f32[2048,256]{0,1:T(8,128)} async-done(((f32[2048,256]{0,1:T(8,128)}), f32[2048,256]{0,1:T(8,128)}) %all-reduce.6.cloned.1.call-update) | async-done | bytes 2097168 | tf_op jit(solution)/shard_map/psum | solution.py:27
  105.0 3.1 %convolution_bitcast_fusion.1 = f32[512,256]{0,1:T(8,128)} fusion(bf16[512,2048]{1,0:T(8,128)(2,1)S(1)} %copy-done, f32[2048,256]{0,1:T(8,128)} %all-reduce.6.cloned.1.call-done), kind=kOutput, calls=%fused_computation.4 | convolution fusion | flops 537919488 | bytes 4718592 | tf_op jit(solution)/shard_map/dot_general | solution.py:29
  108.1 0.0 all-reduce.8.cloned.1.call-update
  108.1 0.2 all-reduce.10.cloned.1.call-start
  108.4 37.4 %all-reduce.8.cloned.1.call-done = f32[512,256]{0,1:T(8,128)} async-done(((f32[512,256]{0,1:T(8,128)}), f32[512,256]{0,1:T(8,128)}) %all-reduce.8.cloned.1.call-update) | async-done | bytes 524304 | tf_op jit(solution)/shard_map/psum | solution.py:30
  145.8 2.5 fusion.17
  148.3 0.0 all-reduce.10.cloned.1.call-update
  148.4 0.0 copy-start.1
  148.4 54.6 %all-reduce.10.cloned.1.call-done = f32[256,256]{0,1:T(8,128)} async-done(((f32[256,256]{0,1:T(8,128)}), f32[256,256]{0,1:T(8,128)}) %all-reduce.10.cloned.1.call-update) | async-done | bytes 262160 | tf_op jit(solution)/shard_map/psum | solution.py:34
  203.0 1.1 copy.5
  204.1 1.0 fusion.3
  205.1 11.7 %cholesky.50 = f32[128,128]{1,0:T(8,128)S(1)} custom-call(f32[128,128]{1,0:T(8,128)S(1)} %cholesky.118), custom_call_target="Cholesky" | custom-call | tf_op jit(solution)/shard_map/jit(cholesky)/cholesky | solution.py:35
  216.8 9.8 %custom-call.15 = f32[1,128,128]{1,2,0:T(8,128)S(1)} custom-call(f32[1,128,128]{2,1,0:T(8,128)S(1)} %get-tuple-element.27), custom_call_target="InvertDiagBlocksLowerTriangular" | custom-call | tf_op jit(solution)/shard_map/jit(cholesky)/cholesky | solution.py:35
  226.7 0.2 constant_dynamic-update-slice_fusion
  226.9 0.3 convolution_subtract_fusion.1
  227.2 11.7 %cholesky.105 = f32[128,128]{1,0:T(8,128)S(1)} custom-call(f32[128,128]{1,0:T(8,128)S(1)} %convolution_subtract_fusion.1), custom_call_target="Cholesky" | custom-call | tf_op jit(solution)/shard_map/jit(cholesky)/cholesky | solution.py:35
  238.9 0.7 compare_reduce_fusion
  241.0 0.1 triangular_solve.57
  241.1 4.3 %while.1 = (s32[]{:T(128)}, f32[256,256]{1,0:T(8,128)S(1)}, s32[2,2]{1,0:T(2,128)S(1)}, f32[2,128,128]{2,1,0:T(8,128)S(1)}, s32[]{:T(128)}) while((s32[]{:T(128)}, f32[256,256]{1,0:T(8,128)S(1)}, s32[2,2]{1,0:T(2,128)S(1)}, f32[2,128,128]{2,1,0:T(8,128)S(1)}, s32[]{:T(128)}) %tuple.29), condition=%wide.while_cond, body=%wide.while_body.sunk | while | flops 2 | bytes 131181 | solution.py:8
  241.3 0.6 fusion.30
  241.9 1.4 bitcast_dynamic-update-slice_fusion.2
  243.3 0.6 fusion.30
  243.9 1.4 bitcast_dynamic-update-slice_fusion.2
  245.4 0.0 copy-start.2
  245.4 0.6 copy-done.2
  246.0 20.5 %custom-call.16 = f32[2,128,128]{1,2,0:T(8,128)S(1)} custom-call(f32[2,128,128]{2,1,0:T(8,128)} %copy-done.2), custom_call_target="InvertDiagBlocksLowerTriangular" | custom-call | tf_op jit(solution)/shard_map/jit(_solve_triangular)/triangular_solve | solution.py:8
  266.5 0.0 copy-done.1
  266.5 0.4 fusion.1
  267.0 0.4 convolution_subtract_fusion
  267.3 0.4 fusion.10
  267.8 0.8 copy.6
  268.6 0.7 fusion.8
  (9 shorter events, 0.2 us)
Async XLA Ops:
  7.2 1.6 copy-start
  7.2 97.8 %all-reduce.6.cloned.1.call-start = ((), (), s32[]{:S(2)}) async-start(), calls=%async_computation | async-start | bytes 4194304 | tf_op jit(solution)/shard_map/psum | solution.py:27
  44.9 101.0 %all-reduce.8.cloned.1.call-start = ((), (), s32[]{:S(2)}) async-start(), calls=%async_computation.1 | async-start | bytes 1048576 | tf_op jit(solution)/shard_map/psum | solution.py:30
  108.1 94.8 %all-reduce.10.cloned.1.call-start = ((), (), s32[]{:S(2)}) async-start(), calls=%async_computation.2 | async-start | bytes 524288 | tf_op jit(solution)/shard_map/psum | solution.py:34
  148.4 118.2 %copy-start.1 = (f32[512,256]{0,1:T(8,128)S(1)}, f32[512,256]{0,1:T(8,128)}, u32[]{:S(2)}) copy-start(f32[512,256]{0,1:T(8,128)} %all-reduce.8.cloned.1.call-done) | copy-start | bytes 1572868
  245.4 0.7 copy-start.2
Sparse Core Ops, SparseCore 0:
  45.0 59.9 all-reduce.5
  108.3 37.4 all-reduce.7
  149.4 53.5 all-reduce.9
where the time goes:
time: 276 us
  waiting for transfers between devices  152 us (55%)
  other arithmetic  56.2 us (20%)
  blocking collectives  32.1 us (12%)
  between operations  15.2 us (6%)
  matrix products  11.3 us (4%)
  local copies, waits for them, and re-layouts  8.27 us (3%)
    psum x1, waiting for transfers between devices, shards(): summed = lax.psum(partial_normal, ('outer', 'inner'))  60.1 us
    psum x1, waiting for transfers between devices, shards(): gram = lax.psum(local_gram, ('outer', 'inner'))  54.6 us
    psum x1, waiting for transfers between devices, shards(): image = lax.psum(partial_image, 'col')  37.4 us
    another operation x6, other arithmetic, shards(): lower = jnp.linalg.cholesky(gram)  34 us
    psum x1, blocking collectives, shards(): sketch = lax.psum(partial_sketch, 'col').astype(jnp.bfloat16)  32.1 us
    another operation x2, other arithmetic, right_solve(): return jax.scipy.linalg.solve_triangular(lower, matrix.T, lower=True).T  20.5 us
  transfers between devices with their start and end apart: 3, of which 3 were waited for; matrix products, arithmetic and copies ran while one was open for 0% of the time, Pallas kernels for 0%

commit v1 on v0

--- a/solution.py
+++ b/solution.py
@@ -31,7 +31,9 @@
     local_gram = jnp.dot(
         image.T, image, precision=lax.Precision.HIGHEST, preferred_element_type=jnp.float32
     )
-    gram = lax.psum(local_gram, ("outer", "inner"))
+    gram = local_gram
+    for name in ("inner", "outer"):
+        gram = lax.psum(gram, name)
     lower = jnp.linalg.cholesky(gram)
     width = image.shape[1] // col_groups
     orthonormal = right_solve(lower, image)

time: 276 us -> 287 us (1.040)
  waiting for transfers between devices: 152 us -> 163 us
    psum x1 -> x2, waiting for transfers between devices: 54.6 us -> 65.5 us  [shards(): gram = lax.psum(gram, name)]
  transfers between devices with their start and end apart: 3 -> 4, of which waited for: 3 -> 4; matrix products, arithmetic and copies ran while one was open for 0% -> 0% of each run, Pallas kernels for 0% -> 0%
where the time goes in v1:
time: 287 us
  waiting for transfers between devices  163 us (57%)
  other arithmetic  56.2 us (20%)
  blocking collectives  32.1 us (11%)
  between operations  15.3 us (5%)
  matrix products  11.3 us (4%)
  local copies, waits for them, and re-layouts  8.27 us (3%)
    psum x2, waiting for transfers between devices, shards(): gram = lax.psum(gram, name)  65.5 us
    psum x1, waiting for transfers between devices, shards(): summed = lax.psum(partial_normal, ('outer', 'inner'))  60.1 us
    psum x1, waiting for transfers between devices, shards(): image = lax.psum(partial_image, 'col')  37.6 us
    another operation x6, other arithmetic, shards(): lower = jnp.linalg.cholesky(gram)  34 us
    psum x1, blocking collectives, shards(): sketch = lax.psum(partial_sketch, 'col').astype(jnp.bfloat16)  32.1 us
    another operation x2, other arithmetic, right_solve(): return jax.scipy.linalg.solve_triangular(lower, matrix.T, lower=True).T  20.5 us
  transfers between devices with their start and end apart: 4, of which 4 were waited for; matrix products, arithmetic and copies ran while one was open for 0% of the time, Pallas kernels for 0%

profile of v1, /device:TPU:0, one launch (start us, length us, event | category | flops | bytes accessed | tf_op | source)
XLA Modules:
  0.0 287.0 jit_solution(14873162181937112885)
XLA Ops:
  7.2 0.0 copy-start
  7.2 0.0 all-reduce.7.cloned.1.call-start
  7.2 1.5 copy-done
  8.8 1.9 fusion.16
  10.7 32.1 %all-reduce.14 = bf16[512,256]{1,0:T(8,128)(2,1)S(1)} all-reduce(f32[512,256]{1,0:T(8,128)S(1)} %fusion.16), channel_id=1, replica_groups=mesh['outer'=4,'inner'=2,'col'=4] {'col'}, use_global_device_ids=true, to_apply=%region_0.0 | all-reduce | flops 131072 | bytes 786432 | tf_op jit(solution)/shard_map/psum | solution.py:25
  42.8 2.0 convolution_bitcast_fusion
  44.8 0.0 all-reduce.7.cloned.1.call-update
  44.9 0.0 all-reduce.9.cloned.1.call-start
  44.9 60.1 %all-reduce.7.cloned.1.call-done = f32[2048,256]{0,1:T(8,128)} async-done(((f32[2048,256]{0,1:T(8,128)}), f32[2048,256]{0,1:T(8,128)}) %all-reduce.7.cloned.1.call-update) | async-done | bytes 2097168 | tf_op jit(solution)/shard_map/psum | solution.py:27
  105.0 3.1 %convolution_bitcast_fusion.1 = f32[512,256]{0,1:T(8,128)} fusion(bf16[512,2048]{1,0:T(8,128)(2,1)S(1)} %copy-done, f32[2048,256]{0,1:T(8,128)} %all-reduce.7.cloned.1.call-done), kind=kOutput, calls=%fused_computation.4 | convolution fusion | flops 537919488 | bytes 4718592 | tf_op jit(solution)/shard_map/dot_general | solution.py:29
  108.1 0.0 all-reduce.9.cloned.1.call-update
  108.1 0.0 all-reduce.11.cloned.1.call-start
  108.2 37.6 %all-reduce.9.cloned.1.call-done = f32[512,256]{0,1:T(8,128)} async-done(((f32[512,256]{0,1:T(8,128)}), f32[512,256]{0,1:T(8,128)}) %all-reduce.9.cloned.1.call-update) | async-done | bytes 524304 | tf_op jit(solution)/shard_map/psum | solution.py:30
  145.8 2.5 fusion.17
  148.3 0.0 all-reduce.11.cloned.1.call-update
  148.3 0.2 all-reduce.13.cloned.1.call-start
  148.6 18.4 %all-reduce.11.cloned.1.call-done = f32[256,256]{0,1:T(8,128)} async-done(((f32[256,256]{0,1:T(8,128)}), f32[256,256]{0,1:T(8,128)}) %all-reduce.11.cloned.1.call-update) | async-done | bytes 262160 | tf_op jit(solution)/shard_map/psum | solution.py:36
  167.0 0.0 all-reduce.13.cloned.1.call-update
  167.0 0.0 copy-start.1
  167.0 47.1 %all-reduce.13.cloned.1.call-done = f32[256,256]{0,1:T(8,128)} async-done(((f32[256,256]{0,1:T(8,128)}), f32[256,256]{0,1:T(8,128)}) %all-reduce.13.cloned.1.call-update) | async-done | bytes 262160 | tf_op jit(solution)/shard_map/psum | solution.py:36
  214.2 1.1 copy.5
  215.2 1.0 fusion.3
  216.2 11.7 %cholesky.50 = f32[128,128]{1,0:T(8,128)S(1)} custom-call(f32[128,128]{1,0:T(8,128)S(1)} %cholesky.118), custom_call_target="Cholesky" | custom-call | tf_op jit(solution)/shard_map/jit(cholesky)/cholesky | solution.py:37
  228.0 9.8 %custom-call.15 = f32[1,128,128]{1,2,0:T(8,128)S(1)} custom-call(f32[1,128,128]{2,1,0:T(8,128)S(1)} %get-tuple-element.27), custom_call_target="InvertDiagBlocksLowerTriangular" | custom-call | tf_op jit(solution)/shard_map/jit(cholesky)/cholesky | solution.py:37
  237.8 0.2 constant_dynamic-update-slice_fusion
  238.0 0.3 convolution_subtract_fusion.1
  238.3 11.7 %cholesky.105 = f32[128,128]{1,0:T(8,128)S(1)} custom-call(f32[128,128]{1,0:T(8,128)S(1)} %convolution_subtract_fusion.1), custom_call_target="Cholesky" | custom-call | tf_op jit(solution)/shard_map/jit(cholesky)/cholesky | solution.py:37
  250.1 0.7 compare_reduce_fusion
  252.2 0.1 triangular_solve.57
  252.3 4.3 %while.1 = (s32[]{:T(128)}, f32[256,256]{1,0:T(8,128)S(1)}, s32[2,2]{1,0:T(2,128)S(1)}, f32[2,128,128]{2,1,0:T(8,128)S(1)}, s32[]{:T(128)}) while((s32[]{:T(128)}, f32[256,256]{1,0:T(8,128)S(1)}, s32[2,2]{1,0:T(2,128)S(1)}, f32[2,128,128]{2,1,0:T(8,128)S(1)}, s32[]{:T(128)}) %tuple.29), condition=%wide.while_cond, body=%wide.while_body.sunk | while | flops 2 | bytes 131181 | solution.py:8
  252.4 0.6 fusion.30
  253.0 1.4 bitcast_dynamic-update-slice_fusion.2
  254.5 0.6 fusion.30
  255.1 1.4 bitcast_dynamic-update-slice_fusion.2
  256.5 0.0 copy-start.2
  256.6 0.6 copy-done.2
  257.2 20.5 %custom-call.16 = f32[2,128,128]{1,2,0:T(8,128)S(1)} custom-call(f32[2,128,128]{2,1,0:T(8,128)} %copy-done.2), custom_call_target="InvertDiagBlocksLowerTriangular" | custom-call | tf_op jit(solution)/shard_map/jit(_solve_triangular)/triangular_solve | solution.py:8
  277.7 0.0 copy-done.1
  277.7 0.4 fusion.1
  278.1 0.4 convolution_subtract_fusion
  278.5 0.4 fusion.10
  278.9 0.8 copy.6
  279.8 0.7 fusion.8
  (9 shorter events, 0.2 us)
Async XLA Ops:
  7.2 1.6 copy-start
  7.2 97.8 %all-reduce.7.cloned.1.call-start = ((), (), s32[]{:S(2)}) async-start(), calls=%async_computation | async-start | bytes 4194304 | tf_op jit(solution)/shard_map/psum | solution.py:27
  44.9 101.0 %all-reduce.9.cloned.1.call-start = ((), (), s32[]{:S(2)}) async-start(), calls=%async_computation.1 | async-start | bytes 1048576 | tf_op jit(solution)/shard_map/psum | solution.py:30
  108.1 58.8 %all-reduce.11.cloned.1.call-start = ((), (), s32[]{:S(2)}) async-start(), calls=%async_computation.2 | async-start | bytes 524288 | tf_op jit(solution)/shard_map/psum | solution.py:36
  148.3 65.8 %all-reduce.13.cloned.1.call-start = ((), (), s32[]{:S(2)}) async-start(), calls=%async_computation.3 | async-start | bytes 524288 | tf_op jit(solution)/shard_map/psum | solution.py:36
  167.0 110.7 %copy-start.1 = (f32[512,256]{0,1:T(8,128)S(1)}, f32[512,256]{0,1:T(8,128)}, u32[]{:S(2)}) copy-start(f32[512,256]{0,1:T(8,128)} %all-reduce.9.cloned.1.call-done) | copy-start | bytes 1572868
  256.5 0.7 copy-start.2
Sparse Core Ops, SparseCore 0:
  45.0 59.9 all-reduce.6
  108.3 37.4 all-reduce.8
  148.7 18.2 all-reduce.10
  170.0 44.0 all-reduce.12

commit v2 on v0

--- a/solution.py
+++ b/solution.py
@@ -31,7 +31,8 @@
     local_gram = jnp.dot(
         image.T, image, precision=lax.Precision.HIGHEST, preferred_element_type=jnp.float32
     )
-    gram = lax.psum(local_gram, ("outer", "inner"))
+    shards_2 = lax.all_gather(local_gram, ("outer", "inner"), axis=0, tiled=False)
+    gram = shards_2.sum(axis=0)
     lower = jnp.linalg.cholesky(gram)
     width = image.shape[1] // col_groups
     orthonormal = right_solve(lower, image)

time: 276 us -> 249 us (0.902)
  waiting for transfers between devices: 152 us -> 126 us
    psum x1 -> x0, waiting for transfers between devices: 54.6 us -> none  [shards(): gram = lax.psum(local_gram, ('outer', 'inner'))]
    all_gather x0 -> x1, waiting for transfers between devices: none -> 28 us  [shards(): lax.all_gather(local_gram, ('outer', 'inner'), axis=0, tiled=False)]
where the time goes in v2:
time: 249 us
  waiting for transfers between devices  126 us (51%)
  other arithmetic  57 us (23%)
  blocking collectives  32.1 us (13%)
  between operations  15.3 us (6%)
  matrix products  11.3 us (5%)
  local copies, waits for them, and re-layouts  7.32 us (3%)
    psum x1, waiting for transfers between devices, shards(): summed = lax.psum(partial_normal, ('outer', 'inner'))  60.1 us
    psum x1, waiting for transfers between devices, shards(): image = lax.psum(partial_image, 'col')  37.4 us
    another operation x6, other arithmetic, shards(): lower = jnp.linalg.cholesky(gram)  34 us
    psum x1, blocking collectives, shards(): sketch = lax.psum(partial_sketch, 'col').astype(jnp.bfloat16)  32.1 us
    all_gather x1, waiting for transfers between devices, shards(): lax.all_gather(local_gram, ('outer', 'inner'), axis=0, tiled=False)  28 us
    another operation x2, other arithmetic, right_solve(): return jax.scipy.linalg.solve_triangular(lower, matrix.T, lower=True).T  20.5 us
  transfers between devices with their start and end apart: 3, of which 3 were waited for; matrix products, arithmetic and copies ran while one was open for 0% of the time, Pallas kernels for 0%

profile of v2, /device:TPU:0, one launch (start us, length us, event | category | flops | bytes accessed | tf_op | source)
XLA Modules:
  0.0 249.1 jit_solution(74896798430342276)
XLA Ops:
  7.2 0.0 copy-start
  7.2 0.0 all-reduce.5.cloned.1.call-start
  7.2 1.5 copy-done
  8.8 1.9 fusion.16
  10.7 32.1 %all-reduce.8 = bf16[512,256]{1,0:T(8,128)(2,1)S(1)} all-reduce(f32[512,256]{1,0:T(8,128)S(1)} %fusion.16), channel_id=1, replica_groups=mesh['outer'=4,'inner'=2,'col'=4] {'col'}, use_global_device_ids=true, to_apply=%region_0.0 | all-reduce | flops 131072 | bytes 786432 | tf_op jit(solution)/shard_map/psum | solution.py:25
  42.8 2.0 convolution_bitcast_fusion
  44.8 0.0 all-reduce.5.cloned.1.call-update
  44.9 0.0 all-reduce.7.cloned.1.call-start
  44.9 60.1 %all-reduce.5.cloned.1.call-done = f32[2048,256]{0,1:T(8,128)} async-done(((f32[2048,256]{0,1:T(8,128)}), f32[2048,256]{0,1:T(8,128)}) %all-reduce.5.cloned.1.call-update) | async-done | bytes 2097168 | tf_op jit(solution)/shard_map/psum | solution.py:27
  105.0 3.2 %convolution_bitcast_fusion.1 = f32[512,256]{0,1:T(8,128)} fusion(bf16[512,2048]{1,0:T(8,128)(2,1)S(1)} %copy-done, f32[2048,256]{0,1:T(8,128)} %all-reduce.5.cloned.1.call-done), kind=kOutput, calls=%fused_computation.4 | convolution fusion | flops 537919488 | bytes 4718592 | tf_op jit(solution)/shard_map/dot_general | solution.py:29
  108.1 0.0 all-reduce.7.cloned.1.call-update
  108.2 0.2 all-gather.3.cloned.1.call-start
  108.4 37.4 %all-reduce.7.cloned.1.call-done = f32[512,256]{0,1:T(8,128)} async-done(((f32[512,256]{0,1:T(8,128)}), f32[512,256]{0,1:T(8,128)}) %all-reduce.7.cloned.1.call-update) | async-done | bytes 524304 | tf_op jit(solution)/shard_map/psum | solution.py:30
  145.8 2.5 %fusion.17 = f32[256,256]{1,0:T(8,128)} fusion(f32[512,256]{0,1:T(8,128)} %all-reduce.7.cloned.1.call-done), kind=kOutput, calls=%fused_computation.42 | convolution fusion | flops 402653184 | bytes 786432 | tf_op jit(solution)/shard_map/dot_general | solution.py:31
  148.3 0.0 all-gather.3.cloned.1.call-update
  148.4 28.0 %all-gather.3.cloned.1.call-done = f32[2048,256]{1,0:T(8,128)} async-done(((f32[256,256]{1,0:T(8,128)}), f32[2048,256]{1,0:T(8,128)}) %all-gather.3.cloned.1.call-update) | async-done | bytes 2097168 | tf_op jit(solution)/shard_map/all_gather | solution.py:34
  176.4 1.8 reduce_sum.9
  178.2 0.0 copy-start.1
  178.2 0.1 copy.6
  178.4 11.7 %cholesky.50 = f32[128,128]{1,0:T(8,128)S(1)} custom-call(f32[128,128]{1,0:T(8,128)S(1)} %cholesky.118), custom_call_target="Cholesky" | custom-call | tf_op jit(solution)/shard_map/jit(cholesky)/cholesky | solution.py:36
  190.1 9.8 %custom-call.15 = f32[1,128,128]{1,2,0:T(8,128)S(1)} custom-call(f32[1,128,128]{2,1,0:T(8,128)S(1)} %get-tuple-element.29), custom_call_target="InvertDiagBlocksLowerTriangular" | custom-call | tf_op jit(solution)/shard_map/jit(cholesky)/cholesky | solution.py:36
  200.0 0.2 constant_dynamic-update-slice_fusion
  200.2 0.3 convolution_subtract_fusion.1
  200.4 11.7 %cholesky.105 = f32[128,128]{1,0:T(8,128)S(1)} custom-call(f32[128,128]{1,0:T(8,128)S(1)} %convolution_subtract_fusion.1), custom_call_target="Cholesky" | custom-call | tf_op jit(solution)/shard_map/jit(cholesky)/cholesky | solution.py:36
  212.2 0.7 compare_reduce_fusion
  214.3 0.1 triangular_solve.57
  214.4 4.3 %while.1 = (s32[]{:T(128)}, f32[256,256]{1,0:T(8,128)S(1)}, s32[2,2]{1,0:T(2,128)S(1)}, f32[2,128,128]{2,1,0:T(8,128)S(1)}, s32[]{:T(128)}) while((s32[]{:T(128)}, f32[256,256]{1,0:T(8,128)S(1)}, s32[2,2]{1,0:T(2,128)S(1)}, f32[2,128,128]{2,1,0:T(8,128)S(1)}, s32[]{:T(128)}) %tuple.30), condition=%wide.while_cond, body=%wide.while_body.sunk | while | flops 2 | bytes 131181 | solution.py:8
  214.6 0.6 fusion.30
  215.2 1.4 bitcast_dynamic-update-slice_fusion.2
  216.6 0.6 fusion.30
  217.2 1.4 bitcast_dynamic-update-slice_fusion.2
  218.6 0.0 copy-start.2
  218.7 0.6 copy-done.2
  219.3 20.5 %custom-call.16 = f32[2,128,128]{1,2,0:T(8,128)S(1)} custom-call(f32[2,128,128]{2,1,0:T(8,128)} %copy-done.2), custom_call_target="InvertDiagBlocksLowerTriangular" | custom-call | tf_op jit(solution)/shard_map/jit(_solve_triangular)/triangular_solve | solution.py:8
  239.8 0.0 copy-done.1
  239.8 0.4 fusion.1
  240.2 0.4 convolution_subtract_fusion
  240.6 0.4 fusion.10
  241.0 0.8 copy.7
  241.9 0.7 fusion.8
  (10 shorter events, 0.2 us)
Async XLA Ops:
  7.2 1.6 copy-start
  7.2 97.8 %all-reduce.5.cloned.1.call-start = ((), (), s32[]{:S(2)}) async-start(), calls=%async_computation | async-start | bytes 4194304 | tf_op jit(solution)/shard_map/psum | solution.py:27
  44.9 101.0 %all-reduce.7.cloned.1.call-start = ((), (), s32[]{:S(2)}) async-start(), calls=%async_computation.1 | async-start | bytes 1048576 | tf_op jit(solution)/shard_map/psum | solution.py:30
  108.2 68.2 %all-gather.3.cloned.1.call-start = ((), (), s32[]{:S(2)}) async-start(), calls=%async_computation.2 | async-start | bytes 2359296 | tf_op jit(solution)/shard_map/all_gather | solution.py:34
  178.2 61.6 %copy-start.1 = (f32[512,256]{0,1:T(8,128)S(1)}, f32[512,256]{0,1:T(8,128)}, u32[]{:S(2)}) copy-start(f32[512,256]{0,1:T(8,128)} %all-reduce.7.cloned.1.call-done) | copy-start | bytes 1572868
  218.6 0.7 copy-start.2
Sparse Core Ops, SparseCore 0:
  45.0 59.9 all-reduce.4
  108.3 37.4 all-reduce.6
  148.5 27.8 all-gather.2
